TPU v7x, 256 devices: a whole 4x4x8 slice. The times are simulated.
256 devices in a mesh: seq: 64 (over y, z, core), mp: 4 (over x).
Axes of the slice: x: 4, y: 4, z: 8, core: 2. Of those that a mesh axis runs over, the one named last changes fastest.
Arguments:
- tokens: bfloat16 [8192, 3584], P('seq'), may hold values from -6 to 6
- query_weight: bfloat16 [3584, 4096], P('seq', 'mp'), may hold values from -0.09375 to 0.09375
- key_weight: bfloat16 [3584, 4096], P('seq', 'mp'), may hold values from -0.09375 to 0.09375
- value_weight: bfloat16 [3584, 4096], P('seq', 'mp'), may hold values from -0.09375 to 0.09375
- adapter_down_maps: bfloat16 [3584, 128], replicated, may hold values from -0.09375 to 0.09375
- lifting_matrices: bfloat16 [2, 64, 4096], P(None, None, 'mp'), may hold values from -0.75 to 0.75
- decay_logarithms: float32 [32, 8192], P('mp', 'seq'), may hold values from -1 to 0, as said below
- output_gradient: bfloat16 [8192, 4096], P('seq', 'mp'), may hold values from -0.06591797 to 0.06591797
Outputs:
- grad_down: float32 [3584, 128], P(('seq', 'mp'))
- grad_up: float32 [2, 64, 4096], P(None, None, 'mp')
Inputs may be any that keep to these rules, and one draw needn't show every extreme that they name: `decay_logarithms`: every entry is negative.
All inputs are finite; a program needn't handle non-finite values.
Results may differ from a plain program's by a relative error of at most 0.006.
Values may be sent and summed in bfloat16 or wider, within the bound.
No kernel may reach another device: no remote copies, remote signals or barrier semaphores. Data moves between devices by JAX's collectives and lax.ppermute only.
A program may use at most 192 MiB of HBM per device.

v0:
```python
import jax
import jax.numpy as jnp
from jax import lax
from jax.experimental import pallas as pl
from jax.experimental.pallas import tpu as pltpu
from jax.sharding import Mesh, PartitionSpec as P


bf16, f32 = jnp.bfloat16, jnp.float32
adapter_scale = 2.0
eps_norm = 1e-06
VMEM = pl.BlockSpec(memory_space=pltpu.VMEM)
SMEM = pl.BlockSpec(memory_space=pltpu.SMEM)
ANY = pl.BlockSpec(memory_space=pl.ANY)


def dot(a, b):
    return jnp.dot(a, b, preferred_element_type=f32)


def dot_t(a, b):
    return lax.dot_general(a, b, (((1,), (1,)), ((), ())), preferred_element_type=f32)


def t_dot(a, b):
    return lax.dot_general(a, b, (((0,), (0,)), ((), ())), preferred_element_type=f32)


def shape(dims, dtype=bf16):
    return jax.ShapeDtypeStruct(dims, dtype)


HBM = pl.BlockSpec(memory_space=pltpu.MemorySpace.HBM)


def call(kernel, outs, *args, mib=6, specs=None, out_specs=None, scratch=()):
    return pl.pallas_call(
        kernel,
        out_shape=outs,
        in_specs=specs or [VMEM] * len(args),
        out_specs=out_specs or jax.tree.map(lambda _: VMEM, outs),
        scratch_shapes=scratch,
        compiler_params=pltpu.CompilerParams(vmem_limit_bytes=mib << 20),
    )(*args)


def begin(pairs, sems, first=0):
    copies = [pltpu.make_async_copy(s, d, sems.at[first + i]) for i, (s, d) in enumerate(pairs)]
    for copy in copies:
        copy.start()
    return copies


def split3(d):
    hi = d.astype(bf16).astype(f32)
    mid = (d - hi).astype(bf16).astype(f32)
    return hi, mid, (d - hi - mid).astype(bf16).astype(f32)


def running(logs):
    chunks, n = logs.shape
    parts = jnp.concatenate(list(split3(logs)) + [jnp.zeros((16 - 3 * chunks, n), f32)], axis=0)
    ones = lax.broadcasted_iota(jnp.int32, (n, n), 0) <= lax.broadcasted_iota(jnp.int32, (n, n), 1)
    sums = dot(parts.astype(bf16), ones.astype(f32).astype(bf16))
    return sums[:chunks] + (sums[chunks : 2 * chunks] + sums[2 * chunks : 3 * chunks])


def down_rows(row):
    return jnp.broadcast_to(row, (128, row.shape[1])).T


def pack_kernel(a_hbm, b_hbm, c_hbm, grad_hbm, decay_hbm, out, a, b, c, grad, decay, sems):
    src = (decay_hbm, grad_hbm, a_hbm, b_hbm, c_hbm)
    copies = begin(list(zip(src, (decay, grad, a, b, c))), sems)
    for copy in copies:
        copy.wait()
    hi, mid, lo = split3(decay[...])
    zero = jnp.zeros((13, 128), f32)
    for h in range(out.shape[0]):
        lanes = slice(h * 128, h * 128 + 128)
        out[h, 0:48, 0:128] = grad[0:48, lanes]
        out[h, 0:48, 128:256] = grad[48:96, lanes]
        out[h, 0:32, 256:384] = grad[96:128, lanes]
        logs = jnp.concatenate([hi[h : h + 1], mid[h : h + 1], lo[h : h + 1], zero], axis=0)
        out[h, 32:48, 256:384] = logs.astype(bf16)
        for i, m in enumerate((a, b, c)):
            out[h, 48:, i * 128 : (i + 1) * 128] = m[:, lanes]


def project_kernel(ids, down, *rest):
    weights, pieces, rest = rest[:9], rest[9:19], rest[19:]
    lift, logs, kvql_hbm, qpre_hbm, tok_hbm, send, wbuf, tok, kvql, qpre, tail, sems = rest
    ny, nz, _, wide = wbuf.shape
    y, c, z = ids[0], ids[1], ids[2]
    width = tok.shape[2]
    pairs = [(down, wbuf.at[:, :, :, wide - 128 :])]
    for i, p in enumerate(weights):
        shift = (0, -1, 1, -2, 2, -3, 3, 4, 4)[i]
        src = lax.rem(z + shift + nz, nz)
        span = (slice(0, ny), slice(0, ny // 2), slice(ny // 2, ny))[max(0, i - 6)]
        pairs.append((p, wbuf.at[span, src, :, : wide - 128]))
    half = tok.shape[1] // 2
    for i, p in enumerate(pieces):
        rel = (0, 0, ny - 1, ny - 1, 1, 1, 2, 2, 2, 2)[i]
        core = c if i % 2 == 0 else 1 - c
        dst = tok.at[lax.rem(y + rel, ny) * 2 + core]
        if i >= 6:
            dst = dst.at[half * ((i - 6) // 2) : half * ((i - 6) // 2) + half]
        pairs.append((p, dst))
    copies = begin(pairs, sems)
    ends = []
    cum = running(logs[...])
    for n in range(ny):
        sums = down_rows(cum[n : n + 1, :])
        total = sums[255:256, :]
        tail[n] = jnp.exp(total - sums)
        ends += list(split3(total))
    extra = jnp.concatenate(ends + [jnp.zeros((16 - len(ends), 128), f32)], axis=0).astype(bf16)
    send[:, 96:112, :] = jnp.broadcast_to(extra[None], (send.shape[0], 16, 128))
    for i in range(10):
        copies[i].wait()
    stores = []
    for step, (rel, used) in enumerate(
        ((0, (0, 1)), (ny - 1, (2, 3)), (1, (4, 5)), (2, (6, 7, 8, 9)))
    ):
        for i in used:
            copies[10 + i].wait()
        n = lax.rem(y + rel, ny)
        two = pl.ds(n * 2, 2)
        stores += begin([(tok.at[two], tok_hbm.at[two])], sems, 20 + 3 * step)
        acc = dot(tok[two].reshape(256, width), wbuf[...].reshape(width, wide))
        low = acc[:, 384:].astype(bf16)
        u = acc[:, :128]
        k = (u * jax.nn.sigmoid(u)).astype(bf16)
        v = (acc[:, 128:256] + adapter_scale * dot(low, lift[1])).astype(bf16)
        u = acc[:, 256:384] + adapter_scale * dot(low, lift[0])
        q = (u * jax.nn.sigmoid(u)).astype(bf16)
        faded = (k.astype(f32) * tail[n]).astype(bf16)
        local = t_dot(faded, v).astype(bf16).reshape(-1, 16, 128)
        send[:, pl.ds(pl.multiple_of(n * 16, 16), 16), :] = local
        side = t_dot(low, faded)[64:].reshape(-1, 8, 128)
        send[:, pl.ds(pl.multiple_of(64 + n * 8, 8), 8), :] = side.astype(bf16)
        for i, m in enumerate((k, v, q, low)):
            kvql[step, i] = m
        qpre[step] = u
        stores += begin(
            [(kvql.at[step], kvql_hbm.at[n]), (qpre.at[step], qpre_hbm.at[n])], sems, 21 + 3 * step
        )
    for copy in stores:
        copy.wait()


def scan_fwd_kernel(got, out, gains):
    nz, ny = got.shape[0], 4
    logs = got[:, 96:112, :].astype(f32)
    state = jnp.zeros((16, 128), f32)
    side = jnp.zeros((8, 128), f32)
    for y in range(ny):
        for z in range(nz):
            total = logs[z, 3 * y] + (logs[z, 3 * y + 1] + logs[z, 3 * y + 2])
            gain = jnp.exp(total)[None]
            gains[y * nz + z] = gain[0]
            out[z, 16 * y : 16 * y + 16, :] = state.astype(bf16)
            out[z, 64 + 8 * y : 72 + 8 * y, :] = side.astype(bf16)
            state = gain * state + got[z, 16 * y : 16 * y + 16, :].astype(f32)
            side = gain * side + got[z, 64 + 8 * y : 72 + 8 * y, :].astype(f32)


def scan_bwd_kernel(got, gains, out):
    nz, ny = got.shape[0], 4
    state = jnp.zeros((8, 128), f32)
    for y in reversed(range(ny)):
        for z in reversed(range(nz)):
            out[z, 8 * y : 8 * y + 8, :] = state.astype(bf16)
            state = gains[y * nz + z][None] * state + got[z, 8 * y : 8 * y + 8, :].astype(f32)
    up = jnp.sum(got[:, 32:48, :].astype(f32), axis=0).astype(bf16)
    out[:, 32:48, :] = jnp.broadcast_to(up[None], (nz, 16, 128))


def attn_kernel(s_in, lift, logs, kvql_hbm, qpre_hbm, bundle_hbm, send, back_hbm, kvql, qpre, bundle, back, sems):
    ny = kvql.shape[0]
    copies = begin(
        [(kvql_hbm, kvql), (bundle_hbm.at[:, 0:48, :], bundle), (qpre_hbm, qpre)], sems
    )
    cum = running(logs[...])
    square = (cum.shape[1], cum.shape[1])
    causal = lax.broadcasted_iota(jnp.int32, square, 1) <= lax.broadcasted_iota(jnp.int32, square, 0)
    every = range(ny)
    ahead, dec = [], []
    for n in every:
        sums = down_rows(cum[n : n + 1, :])
        ahead.append(jnp.exp(sums))
        spread = jnp.concatenate([sums, sums], axis=1) - cum[n : n + 1, :]
        dec.append(jnp.where(causal, jnp.exp(jnp.where(causal, spread, 0.0)), 0.0))
    s = [s_in[:, n * 16 : n * 16 + 16, :].reshape(128, 128) for n in every]
    side = [
        s_in[:, 64 + n * 8 : 72 + n * 8, :].astype(f32).reshape(64, 128).astype(bf16) for n in every
    ]
    copies[0].wait()
    k, v, q, low = ([kvql[n, i] for n in every] for i in range(4))
    mixed = [(dot_t(q[n], k[n]) * dec[n]).astype(bf16) for n in every]
    attn = [dot(mixed[n], v[n]) + ahead[n] * dot(q[n], s[n]) for n in every]
    copies[1].wait()
    d = []
    for n in every:
        inv = lax.rsqrt(jnp.mean(attn[n] * attn[n], axis=-1, keepdims=True) + eps_norm)
        normed = attn[n] * inv
        parts = []
        for b in (2 * n, 2 * n + 1):
            parts += [bundle[b, :, 0:128], bundle[b, :, 128:256], bundle[b, 0:32, 256:384]]
        up = jnp.concatenate(parts, axis=0).astype(f32)
        dn = (up - normed * jnp.mean(up * normed, axis=-1, keepdims=True)) * inv
        d.append(dn.astype(bf16))
    carried = [t_dot((q[n].astype(f32) * ahead[n]).astype(bf16), d[n]).astype(bf16) for n in every]
    dm = [(dot_t(d[n], v[n]) * dec[n]).astype(bf16) for n in every]
    cross = sum(dot(side[n], carried[n]) for n in every)
    for n in every:
        image = dot_t(lift[1], carried[n])[64:].reshape(-1, 8, 128)
        send[:, n * 8 : n * 8 + 8, :] = image.astype(bf16)
    dv = [t_dot(mixed[n], d[n]).astype(bf16) for n in every]
    dq = [dot(dm[n], k[n]) + ahead[n] * dot_t(d[n], s[n]) for n in every]
    copies[2].wait()
    for n in every:
        u = qpre[n]
        sig = jax.nn.sigmoid(u)
        dq[n] = (dq[n] * (sig * (1.0 + u * (1.0 - sig)))).astype(bf16)
    for n in every:
        back[n] = adapter_scale * (dot_t(dq[n], lift[0]) + dot_t(dv[n], lift[1]))
    store = begin([(back, back_hbm)], sems, 3)[0]
    total_q = sum(t_dot(low[n], dq[n]) for n in every)
    total_v = sum(t_dot(low[n], dv[n]) for n in every)
    up = adapter_scale * jnp.concatenate([total_q[:64], total_v[64:] + cross], axis=0)
    send[:, 32:48, :] = up.astype(bf16).reshape(-1, 16, 128)
    store.wait()


def final_kernel(r_in, logs, kvql_hbm, back_hbm, tok_hbm, out, up, k, back, tok, acc, terms, sems):
    ny = k.shape[0]
    blocks, own, width = tok.shape
    copies = begin([(kvql_hbm.at[:, 0], k), (back_hbm, back)], sems)
    parts = begin([(tok_hbm.at[b], tok.at[b]) for b in range(blocks)], sems, 2)
    cum = running(logs[...])
    tails = []
    for n in range(ny):
        sums = down_rows(cum[n : n + 1, :])
        tails.append(adapter_scale * jnp.exp(sums[255:256, :] - sums))
    rs = []
    for n in range(ny):
        r = r_in[:, n * 8 : n * 8 + 8, :].astype(f32).reshape(64, 128)
        rs.append(jnp.concatenate([jnp.zeros((64, 128), f32), r], axis=0).astype(bf16))
    up[...] = r_in[:, 32:48, :].reshape(128, 128)
    for copy in copies:
        copy.wait()
    small = [(back[n] + tails[n] * dot_t(k[n], rs[n])).T.astype(bf16) for n in range(ny)]
    small = [jnp.concatenate(small[i : i + 2], axis=1) for i in (0, 2)]
    half = blocks // 2
    wide = width // 4
    per = out.shape[1] // 8
    for part in parts[:half]:
        part.wait()
    for y in range(4):
        m = slice(y * wide, y * wide + wide)
        acc[:, m] = dot(small[0], tok[:half, :, m].reshape(half * own, wide))
    for part in parts[half:]:
        part.wait()
    for y in range(4):
        m = slice(y * wide, y * wide + wide)
        terms[m, :] = (acc[:, m] + dot(small[1], tok[half:, :, m].reshape(half * own, wide))).T
        for cx in range(8):
            base = (y * 64 + cx) * per
            rows = [terms[pl.ds(base + r, 8, stride=8 * per), :] for r in range(per)]
            out[y * 8 + cx] = jnp.concatenate(rows, axis=0).astype(bf16)


def fold_kernel(got, out, tmp):
    tmp[...] = jnp.sum(got[...].astype(f32), axis=0)
    nz = out.shape[0]
    per = tmp.shape[0] // nz
    for z in range(nz):
        out[z] = jnp.concatenate(
            [tmp[pl.ds(z, per, stride=nz), :], jnp.zeros((out.shape[1] - per, 128), f32)], axis=0
        ).astype(bf16)


def last_kernel(got, out):
    out[...] = jnp.sum(got[...].astype(f32), axis=0)[: out.shape[0]]


def up_kernel(ids, pair, *rest):
    pieces, out = rest[:-1], rest[-1]
    y, c = ids[0], ids[1]

    def put(yy, cc, val):
        out[:, pl.ds(pl.multiple_of((yy * 2 + cc) * 128, 128), 128)] = val.astype(f32)

    put(y, c, pair[0])
    put(y, 1 - c, pair[1])
    for i, rel in enumerate((3, 1, 2)):
        yy = lax.rem(y + rel, 4)
        put(yy, c, pieces[i][0])
        put(yy, 1 - c, pieces[i][1])


def layer(tokens, wq, wk, wv, down, lift, decay, grad):
    own, width = tokens.shape
    rank = lift.shape[1]
    heads = decay.shape[0]
    hk = wq.shape[1] // heads
    group = ("y", "c")
    ny, nz, nc, nx = (lax.axis_size(a) for a in ("y", "z", "c", "x"))
    ids = jnp.stack([lax.axis_index(a) for a in ("y", "c", "z")]).astype(jnp.int32)
    head = lax.axis_index("y") * nc + lax.axis_index("c")
    rows = wq.shape[0]
    span = nc * own
    ring = lambda v, s, a="y", n=ny: lax.ppermute(v, a, [(i, (i + s) % n) for i in range(n)])
    swap = lambda v: lax.ppermute(v, "c", [(0, 1), (1, 0)])
    DMA = pltpu.SemaphoreType.DMA

    below = ring(tokens, 1)
    above = ring(tokens, -1)
    far0 = ring(below[: own // 2], 1)
    far1 = ring(above[own // 2 :], -1)
    pieces = []
    for p in (tokens, below, above, far0, far1):
        pieces += [p, swap(p)]

    bundle = call(
        pack_kernel, shape((heads, 48 + rows, 3 * hk)), wk, wv, wq, grad, decay,
        specs=[HBM] * 5,
        mib=60,
        scratch=[pltpu.VMEM(wk.shape, bf16)] * 3
        + [pltpu.VMEM(grad.shape, bf16), pltpu.VMEM(decay.shape, f32), DMA((5,))],
    )
    bundle = lax.all_to_all(bundle, group, 0, 0, tiled=True)
    w = bundle[:, 48:].reshape(heads * rows, 3 * hk)
    weights, ahead, behind = [w], w, w
    for _ in range(nz // 2 - 1):
        ahead = ring(ahead, 1, "z", nz)
        behind = ring(behind, -1, "z", nz)
        weights += [ahead, behind]
    half = heads * rows // 2
    weights.append(ring(weights[3][:half], 2, "z", nz))
    weights.append(ring(weights[4][half:], -2, "z", nz))
    deep = nc * rows
    weights = [p.reshape(-1, deep, 3 * hk) for p in weights]

    logs = bundle[:, 32:35, 2 * hk :].astype(f32)
    logs = (logs[:, 0] + (logs[:, 1] + logs[:, 2])).reshape(ny, span)
    lift = lax.dynamic_slice_in_dim(lift, head * hk, hk, 2)
    zero = jnp.zeros((rank, hk), bf16)
    lift = jnp.stack([jnp.concatenate([lift[0], zero]), jnp.concatenate([zero, lift[1]])])

    kvql, qpre, tok, send = call(
        project_kernel,
        (
            shape((ny, 4, span, hk)), shape((ny, span, hk), f32),
            shape((heads, own, width)), shape((nz, 112, hk)),
        ),
        ids, down.reshape(ny, nz, deep, 2 * rank), *weights, *pieces, lift, logs,
        mib=60,
        specs=[SMEM] + [HBM] * 20 + [VMEM] * 2,
        out_specs=(HBM, HBM, HBM, VMEM),
        scratch=[
            pltpu.VMEM((ny, nz, deep, 3 * hk + 2 * rank), bf16),
            pltpu.VMEM((heads, own, width), bf16),
            pltpu.VMEM((ny, 4, span, hk), bf16),
            pltpu.VMEM((ny, span, hk), f32),
            pltpu.VMEM((ny, span, hk), f32),
            DMA((32,)),
        ],
    )

    got = lax.all_to_all(send, "z", 0, 0, tiled=True)
    scanned, gains = call(scan_fwd_kernel, (shape((nz, 96, hk)), shape((nz * ny, hk), f32)), got)
    s_in = lax.all_to_all(scanned, "z", 0, 0, tiled=True)

    send, back = call(
        attn_kernel,
        (shape((nz, 48, hk)), shape((ny, span, hk), f32)),
        s_in, lift, logs, kvql, qpre, bundle,
        mib=60,
        specs=[VMEM] * 3 + [HBM] * 3,
        out_specs=(VMEM, HBM),
        scratch=[
            pltpu.VMEM((ny, 4, span, hk), bf16),
            pltpu.VMEM((ny, span, hk), f32),
            pltpu.VMEM((heads, 48, 3 * hk), bf16),
            pltpu.VMEM((ny, span, hk), f32),
            DMA((4,)),
        ],
    )
    got = lax.all_to_all(send, "z", 0, 0, tiled=True)
    scanned = call(scan_bwd_kernel, shape((nz, 48, hk)), got, gains)
    r_in = lax.all_to_all(scanned, "z", 0, 0, tiled=True)

    out_rows = width // (ny * nz * nc * nx)
    down_terms, up = call(
        final_kernel,
        (shape((ny * nc * nx, nz * out_rows, hk)), shape((2 * rank, hk))),
        r_in, logs, kvql, back, tok,
        specs=[VMEM] * 2 + [HBM] * 3,
        scratch=[
            pltpu.VMEM((ny, span, hk), bf16),
            pltpu.VMEM((ny, span, hk), f32),
            pltpu.VMEM((heads, own, width), bf16),
            pltpu.VMEM((2 * rank, width), f32),
            pltpu.VMEM((width, 2 * rank), f32),
            DMA((10,)),
        ],
        mib=60,
    )
    down_terms = lax.all_to_all(down_terms, ("y", "c", "x"), 0, 0, tiled=True)
    pair = jnp.stack([up, swap(up)])
    ups = [ring(pair, 1), ring(pair, -1), ring(pair, 2)]
    down_terms = call(
        fold_kernel, shape((nz, 16, hk)), down_terms,
        scratch=[pltpu.VMEM((nz * out_rows, hk), f32)],
    )
    down_terms = lax.all_to_all(down_terms, "z", 0, 0, tiled=True)
    grad_down = call(last_kernel, shape((out_rows, hk), f32), down_terms)
    grad_up = call(
        up_kernel, shape((2 * rank, heads * hk), f32), ids, pair, *ups,
        specs=[SMEM] + [VMEM] * 4,
    )
    return (grad_down, grad_up.reshape(2, rank, heads * hk))


def solution(mesh):
    n_mp = mesh.shape["mp"]
    wide = Mesh(mesh.devices.reshape(4, 8, 2, n_mp), ("y", "z", "c", "x"))
    seq = ("y", "z", "c")
    return jax.shard_map(
        layer,
        mesh=wide,
        in_specs=(
            P(seq, None),
            P(seq, "x"),
            P(seq, "x"),
            P(seq, "x"),
            P(),
            P(None, None, "x"),
            P("x", seq),
            P(seq, "x"),
        ),
        out_specs=(P(("y", "z", "c", "x"), None), P(None, None, "x")),
        check_vma=False,
    )
```

profile of v0, /device:TPU:2, one launch (start us, length us, event | category | flops | bytes accessed | tf_op | source)
XLA Modules:
  0.0 194.8 jit_solution(13971471230427062361)
XLA Ops:
  0.6 1.7 collective-permute-start.9
  2.3 1.7 collective-permute-start.11
  3.9 2.1 %shard_map.95 = bf16[8,104,384]{2,1,0:T(8,128)(2,1)} custom-call(bf16[56,1024]{1,0:T(8,128)(2,1)} %a_hbm.1, bf16[56,1024]{1,0:T(8,128)(2,1)} %b_hbm.1, bf16[56,1024]{1,0:T(8,128)(2,1)} %c_hbm.1, bf16[128,1024]{1,0:T(8,128)(2,1)} %grad_hbm.1, f32[8,128]{1,0:T(8,128)} %decay_hbm.1), custom_call_target="tpu_custom_call" | custom-call | tf_op jit(solution)/shard_map/pallas_call | solution.py:37
  6.0 3.6 %all-to-all-start = ((bf16[8,104,384]{2,1,0:T(8,128)(2,1)}), bf16[8,104,384]{2,1,0:T(8,128)(2,1)S(1)}, u32[]{:S(2)}, u32[]{:S(2)}) async-start(bf16[8,104,384]{2,1,0:T(8,128)(2,1)} %shard_map.95), calls=%async_computation | async-start | bytes 1277952 | tf_op jit(solution)/shard_map/all_to_all | solution.py:334
  10.0 22.3 %all-to-all-done.bundle_hbm = bf16[8,104,384]{2,1,0:T(8,128)(2,1)S(1)} async-done(((bf16[8,104,384]{2,1,0:T(8,128)(2,1)}), bf16[8,104,384]{2,1,0:T(8,128)(2,1)S(1)}, u32[]{:S(2)}, u32[]{:S(2)}) %all-to-all-start) | async-done | bytes 639008 | tf_op jit(solution)/shard_map/all_to_all | solution.py:334
  32.4 5.9 %collective-permute-start.1 = (bf16[448,384]{1,0:T(8,128)(2,1)S(1)}, bf16[448,384]{1,0:T(8,128)(2,1)S(1)}, u32[]{:S(2)}, u32[]{:S(2)}) collective-permute-start(bf16[448,384]{1,0:T(8,128)(2,1)S(1)} %bitcast.25), channel_id=1, source_target_pairs={{0,56},{8,0},{16,8},{24,16},{32,24},{40,32},{48,40},{56,48},{1,57}... | collective-permute-start | bytes 1032200 | tf_op jit(solution)/shard_map/ppermute | solution.py:315
  38.3 6.4 %collective-permute-done.1 = bf16[448,384]{1,0:T(8,128)(2,1)S(1)} collective-permute-done((bf16[448,384]{1,0:T(8,128)(2,1)S(1)}, bf16[448,384]{1,0:T(8,128)(2,1)S(1)}, u32[]{:S(2)}, u32[]{:S(2)}) %collective-permute-start.1) | collective-permute-done | bytes 344096 | tf_op jit(solution)/shard_map/ppermute | solution.py:315
  44.7 3.7 %collective-permute-start.3 = (bf16[448,384]{1,0:T(8,128)(2,1)S(1)}, bf16[448,384]{1,0:T(8,128)(2,1)S(1)}, u32[]{:S(2)}, u32[]{:S(2)}) collective-permute-start(bf16[448,384]{1,0:T(8,128)(2,1)S(1)} %collective-permute-done.1), channel_id=1, source_target_pairs={{0,56},{8,0},{16,8},{24,16},{32,24},{40,32},{48,40},{56,48},{1,57}... | collective-permute-start | bytes 1032200 | tf_op jit(solution)/shard_map/ppermute | solution.py:315
  48.4 0.8 slice.47
  49.3 1.1 collective-permute-start.13
  50.4 0.8 slice.48
  51.3 2.1 %collective-permute-start.15 = (bf16[64,3584]{1,0:T(8,128)(2,1)}, bf16[64,3584]{1,0:T(8,128)(2,1)}, u32[]{:S(2)}, u32[]{:S(2)}) collective-permute-start(bf16[64,3584]{1,0:T(8,128)(2,1)} %slice.48), channel_id=1, source_target_pairs={{0,192},{64,0},{128,64},{192,128},{1,193},{65,1},{129,65},{193,129... | collective-permute-start | bytes 1376264 | tf_op jit(solution)/shard_map/ppermute | solution.py:315
  54.0 7.8 %collective-permute-done.2 = bf16[448,384]{1,0:T(8,128)(2,1)S(1)} collective-permute-done((bf16[448,384]{1,0:T(8,128)(2,1)S(1)}, bf16[448,384]{1,0:T(8,128)(2,1)S(1)}, u32[]{:S(2)}, u32[]{:S(2)}) %collective-permute-start.2) | collective-permute-done | bytes 344096 | tf_op jit(solution)/shard_map/ppermute | solution.py:315
  62.0 2.9 %collective-permute-start.6 = (bf16[224,384]{1,0:T(8,128)(2,1)S(1)}, bf16[224,384]{1,0:T(8,128)(2,1)S(1)}, u32[]{:S(2)}, u32[]{:S(2)}) collective-permute-start(bf16[224,384]{1,0:T(8,128)(2,1)S(1)} %slice.45), channel_id=1, source_target_pairs={{0,16},{8,24},{16,32},{24,40},{32,48},{40,56},{48,0},{56,8},{1,17}... | collective-permute-start | bytes 516104 | tf_op jit(solution)/shard_map/ppermute | solution.py:315
  65.7 8.9 %collective-permute-done.7 = bf16[224,384]{1,0:T(8,128)(2,1)S(1)} collective-permute-done((bf16[224,384]{1,0:T(8,128)(2,1)S(1)}, bf16[224,384]{1,0:T(8,128)(2,1)S(1)}, u32[]{:S(2)}, u32[]{:S(2)}) %collective-permute-start.7) | collective-permute-done | bytes 172064 | tf_op jit(solution)/shard_map/ppermute | solution.py:315
  78.4 10.1 %collective-permute-done.4 = bf16[448,384]{1,0:T(8,128)(2,1)} collective-permute-done((bf16[448,384]{1,0:T(8,128)(2,1)S(1)}, bf16[448,384]{1,0:T(8,128)(2,1)}, u32[]{:S(2)}, u32[]{:S(2)}) %collective-permute-start.4) | collective-permute-done | bytes 344096 | tf_op jit(solution)/shard_map/ppermute | solution.py:315
  88.6 10.6 %shard_map.96 = (bf16[4,4,256,128]{3,2,1,0:T(8,128)(2,1)}, f32[4,256,128]{2,1,0:T(8,128)}, bf16[8,128,3584]{2,1,0:T(8,128)(2,1)}, bf16[8,112,128]{2,1,0:T(8,128)(2,1)}) custom-call(s32[3]{0:T(128)} %pad_add_fusion.ids, bf16[4,8,112,128]{3,2,1,0:T(8,128)(2,1)} %bitcast.28, bf16[4,112,384]{2,1,0:T(8,128)(2,1)} %bitcast.27, bf16[4,112,384]{2,1,0:T(8,128)(2,1)} %bitcast.33, ...), custom_call_target="tpu_custom_call" | custom-call | tf_op jit(solution)/shard_map/pallas_call | solution.py:37
  99.2 14.2 %all_to_all.35.got = bf16[8,112,128]{2,1,0:T(8,128)(2,1)S(1)} all-to-all(bf16[8,112,128]{2,1,0:T(8,128)(2,1)} %get-tuple-element.12), channel_id=1, replica_groups=mesh['y'=4,'z'=8,'c'=2,'x'=4] {'z'}, dimensions={0} | all-to-all | bytes 458752 | tf_op jit(solution)/shard_map/all_to_all | solution.py:373
  113.5 12.8 %all_to_all.36.s_in = bf16[8,96,128]{2,1,0:T(8,128)(2,1)} all-to-all(bf16[8,96,128]{2,1,0:T(8,128)(2,1)S(1)} %get-tuple-element.13), channel_id=1, replica_groups=mesh['y'=4,'z'=8,'c'=2,'x'=4] {'z'}, dimensions={0} | all-to-all | bytes 393216 | tf_op jit(solution)/shard_map/all_to_all | solution.py:375
  126.4 5.8 %shard_map.98 = (bf16[8,48,128]{2,1,0:T(8,128)(2,1)}, f32[4,256,128]{2,1,0:T(8,128)}) custom-call(bf16[8,96,128]{2,1,0:T(8,128)(2,1)} %all_to_all.36.s_in, bf16[2,128,128]{2,1,0:T(8,128)(2,1)} %pad_maximum_fusion.rest_19_.lift, f32[4,256]{1,0:T(4,128)} %add.26.rest_20_.logs, bf16[4,4,256,128]{3,2,1,0:T(8,128)(2,1)} %get-tuple-element.14.kvql_hbm, ...), custom_call_target="tpu_custom_call" | custom-call | tf_op jit(solution)/shard_map/pallas_call | solution.py:37
  132.1 12.0 %all_to_all.37.got = bf16[8,48,128]{2,1,0:T(8,128)(2,1)S(1)} all-to-all(bf16[8,48,128]{2,1,0:T(8,128)(2,1)} %get-tuple-element.16), channel_id=1, replica_groups=mesh['y'=4,'z'=8,'c'=2,'x'=4] {'z'}, dimensions={0} | all-to-all | bytes 196608 | tf_op jit(solution)/shard_map/all_to_all | solution.py:392
  144.2 11.8 %all_to_all.38.r_in = bf16[8,48,128]{2,1,0:T(8,128)(2,1)} all-to-all(bf16[8,48,128]{2,1,0:T(8,128)(2,1)S(1)} %shard_map.99), channel_id=1, replica_groups=mesh['y'=4,'z'=8,'c'=2,'x'=4] {'z'}, dimensions={0} | all-to-all | bytes 196608 | tf_op jit(solution)/shard_map/all_to_all | solution.py:394
  156.0 6.7 %shard_map.100 = (bf16[32,112,128]{2,1,0:T(8,128)(2,1)}, bf16[128,128]{1,0:T(8,128)(2,1)}) custom-call(bf16[8,48,128]{2,1,0:T(8,128)(2,1)} %all_to_all.38.r_in, f32[4,256]{1,0:T(4,128)} %add.26.rest_20_.logs, bf16[4,4,256,128]{3,2,1,0:T(8,128)(2,1)} %get-tuple-element.14.kvql_hbm, f32[4,256,128]{2,1,0:T(8,128)} %get-tuple-element.18.back_hbm, ...), custom_call_target="tpu_custom_call" | custom-call | tf_op jit(solution)/shard_map/pallas_call | solution.py:37
  162.7 5.0 %all-to-all-start.5 = ((bf16[32,112,128]{2,1,0:T(8,128)(2,1)}), bf16[32,112,128]{2,1,0:T(8,128)(2,1)S(1)}, u32[]{:S(2)}, u32[]{:S(2)}) async-start(bf16[32,112,128]{2,1,0:T(8,128)(2,1)} %get-tuple-element.20), calls=%async_computation.5 | async-start | bytes 1835008 | tf_op jit(solution)/shard_map/all_to_all | solution.py:412
  167.9 1.3 collective-permute-done.17
  170.0 3.0 %collective-permute-start.20 = (bf16[2,128,128]{2,1,0:T(8,128)(2,1)S(1)}, bf16[2,128,128]{2,1,0:T(8,128)(2,1)S(1)}, u32[]{:S(2)}, u32[]{:S(2)}) collective-permute-start(bf16[2,128,128]{2,1,0:T(8,128)(2,1)S(1)} %pad_maximum_fusion.1.pair), channel_id=1, source_target_pairs={{0,128},{64,192},{128,0},{192,64},{1,129},{65,193},{129,1},{193,65... | collective-permute-start | bytes 196616 | tf_op jit(solution)/shard_map/ppermute | solution.py:315
  172.9 1.2 collective-permute-start.19
  174.1 0.9 collective-permute-start.18
  175.0 7.2 %all-to-all-done.5.got = bf16[32,112,128]{2,1,0:T(8,128)(2,1)S(1)} async-done(((bf16[32,112,128]{2,1,0:T(8,128)(2,1)}), bf16[32,112,128]{2,1,0:T(8,128)(2,1)S(1)}, u32[]{:S(2)}, u32[]{:S(2)}) %all-to-all-start.5) | async-done | bytes 917536 | tf_op jit(solution)/shard_map/all_to_all | solution.py:412
  182.9 3.3 %all-to-all-start.6 = ((bf16[8,16,128]{2,1,0:T(8,128)(2,1)}), bf16[8,16,128]{2,1,0:T(8,128)(2,1)S(1)}, u32[]{:S(2)}, u32[]{:S(2)}) async-start(bf16[8,16,128]{2,1,0:T(8,128)(2,1)} %shard_map.101), calls=%async_computation.6 | async-start | bytes 65536 | tf_op jit(solution)/shard_map/all_to_all | solution.py:419
  186.3 1.4 shard_map.103
  187.7 6.5 %all-to-all-done.6.got = bf16[8,16,128]{2,1,0:T(8,128)(2,1)S(1)} async-done(((bf16[8,16,128]{2,1,0:T(8,128)(2,1)}), bf16[8,16,128]{2,1,0:T(8,128)(2,1)S(1)}, u32[]{:S(2)}, u32[]{:S(2)}) %all-to-all-start.6) | async-done | bytes 32800 | tf_op jit(solution)/shard_map/all_to_all | solution.py:419
  (64 shorter events, 8.4 us)
Async XLA Ops:
  0.6 47.8 %collective-permute-start.9 = (bf16[128,3584]{1,0:T(8,128)(2,1)}, bf16[128,3584]{1,0:T(8,128)(2,1)S(1)}, u32[]{:S(2)}, u32[]{:S(2)}) collective-permute-start(bf16[128,3584]{1,0:T(8,128)(2,1)} %rest_9_.1), channel_id=1, source_target_pairs={{0,64},{64,128},{128,192},{192,0},{1,65},{65,129},{129,193},{193,1... | collective-permute-start | bytes 2752520 | tf_op jit(solution)/shard_map/ppermute | solution.py:315
  2.3 48.1 %collective-permute-start.11 = (bf16[128,3584]{1,0:T(8,128)(2,1)}, bf16[128,3584]{1,0:T(8,128)(2,1)S(1)}, u32[]{:S(2)}, u32[]{:S(2)}) collective-permute-start(bf16[128,3584]{1,0:T(8,128)(2,1)} %rest_9_.1), channel_id=1, source_target_pairs={{0,192},{64,0},{128,64},{192,128},{1,193},{65,1},{129,65},{193,129... | collective-permute-start | bytes 2752520 | tf_op jit(solution)/shard_map/ppermute | solution.py:315
  6.0 26.3 %all-to-all-start = ((bf16[8,104,384]{2,1,0:T(8,128)(2,1)}), bf16[8,104,384]{2,1,0:T(8,128)(2,1)S(1)}, u32[]{:S(2)}, u32[]{:S(2)}) async-start(bf16[8,104,384]{2,1,0:T(8,128)(2,1)} %shard_map.95), calls=%async_computation | async-start | bytes 1277952 | tf_op jit(solution)/shard_map/all_to_all | solution.py:334
  9.6 43.8 %collective-permute-start.8 = (bf16[128,3584]{1,0:T(8,128)(2,1)}, bf16[128,3584]{1,0:T(8,128)(2,1)}, u32[]{:S(2)}, u32[]{:S(2)}) collective-permute-start(bf16[128,3584]{1,0:T(8,128)(2,1)} %rest_9_.1), channel_id=1, source_target_pairs={{0,4},{4,0},{1,5},{5,1},{2,6},{6,2},{3,7},{7,3},{8,12},{12,8},{9,1... | collective-permute-start | bytes 2752520 | tf_op jit(solution)/shard_map/ppermute | solution.py:316
  32.3 66.9 %copy-start.1 = (bf16[8,104,384]{2,1,0:T(8,128)(2,1)}, bf16[8,104,384]{2,1,0:T(8,128)(2,1)S(1)}, u32[]{:S(2)}) copy-start(bf16[8,104,384]{2,1,0:T(8,128)(2,1)S(1)} %all-to-all-done.bundle_hbm) | copy-start | bytes 1916932
  32.3 56.2 %copy-start.4 = (bf16[8,56,384]{2,1,0:T(8,128)(2,1)}, bf16[8,56,384]{2,1,0:T(8,128)(2,1)S(1)}, u32[]{:S(2)}) copy-start(bf16[8,56,384]{2,1,0:T(8,128)(2,1)S(1)} %slice.44) | copy-start | bytes 1032196
  32.4 12.4 %collective-permute-start.1 = (bf16[448,384]{1,0:T(8,128)(2,1)S(1)}, bf16[448,384]{1,0:T(8,128)(2,1)S(1)}, u32[]{:S(2)}, u32[]{:S(2)}) collective-permute-start(bf16[448,384]{1,0:T(8,128)(2,1)S(1)} %bitcast.25), channel_id=1, source_target_pairs={{0,56},{8,0},{16,8},{24,16},{32,24},{40,32},{48,40},{56,48},{1,57}... | collective-permute-start | bytes 1032200 | tf_op jit(solution)/shard_map/ppermute | solution.py:315
  38.3 15.1 %collective-permute-start = (bf16[448,384]{1,0:T(8,128)(2,1)S(1)}, bf16[448,384]{1,0:T(8,128)(2,1)S(1)}, u32[]{:S(2)}, u32[]{:S(2)}) collective-permute-start(bf16[448,384]{1,0:T(8,128)(2,1)S(1)} %bitcast.26), channel_id=1, source_target_pairs={{0,8},{8,16},{16,24},{24,32},{32,40},{40,48},{48,56},{56,0},{1,9},... | collective-permute-start | bytes 1032200 | tf_op jit(solution)/shard_map/ppermute | solution.py:315
  44.7 17.1 %copy-start.7 = (bf16[448,384]{1,0:T(8,128)(2,1)}, bf16[448,384]{1,0:T(8,128)(2,1)S(1)}, u32[]{:S(2)}) copy-start(bf16[448,384]{1,0:T(8,128)(2,1)S(1)} %collective-permute-done.1) | copy-start | bytes 1032196
  44.7 9.3 %collective-permute-start.3 = (bf16[448,384]{1,0:T(8,128)(2,1)S(1)}, bf16[448,384]{1,0:T(8,128)(2,1)S(1)}, u32[]{:S(2)}, u32[]{:S(2)}) collective-permute-start(bf16[448,384]{1,0:T(8,128)(2,1)S(1)} %collective-permute-done.1), channel_id=1, source_target_pairs={{0,56},{8,0},{16,8},{24,16},{32,24},{40,32},{48,40},{56,48},{1,57}... | collective-permute-start | bytes 1032200 | tf_op jit(solution)/shard_map/ppermute | solution.py:315
  48.4 40.1 %copy-start.2 = (bf16[128,3584]{1,0:T(8,128)(2,1)}, bf16[128,3584]{1,0:T(8,128)(2,1)S(1)}, u32[]{:S(2)}) copy-start(bf16[128,3584]{1,0:T(8,128)(2,1)S(1)} %collective-permute-done.9.rest_11_) | copy-start | bytes 2752516
  49.3 12.6 %collective-permute-start.13 = (bf16[64,3584]{1,0:T(8,128)(2,1)}, bf16[64,3584]{1,0:T(8,128)(2,1)}, u32[]{:S(2)}, u32[]{:S(2)}) collective-permute-start(bf16[64,3584]{1,0:T(8,128)(2,1)} %slice.47), channel_id=1, source_target_pairs={{0,64},{64,128},{128,192},{192,0},{1,65},{65,129},{129,193},{193,1... | collective-permute-start | bytes 1376264 | tf_op jit(solution)/shard_map/ppermute | solution.py:315
  50.4 38.1 %copy-start.3 = (bf16[128,3584]{1,0:T(8,128)(2,1)}, bf16[128,3584]{1,0:T(8,128)(2,1)S(1)}, u32[]{:S(2)}) copy-start(bf16[128,3584]{1,0:T(8,128)(2,1)S(1)} %collective-permute-done.11.rest_13_) | copy-start | bytes 2752516
  51.3 10.8 %collective-permute-start.15 = (bf16[64,3584]{1,0:T(8,128)(2,1)}, bf16[64,3584]{1,0:T(8,128)(2,1)}, u32[]{:S(2)}, u32[]{:S(2)}) collective-permute-start(bf16[64,3584]{1,0:T(8,128)(2,1)} %slice.48), channel_id=1, source_target_pairs={{0,192},{64,0},{128,64},{192,128},{1,193},{65,1},{129,65},{193,129... | collective-permute-start | bytes 1376264 | tf_op jit(solution)/shard_map/ppermute | solution.py:315
  53.4 8.5 %collective-permute-start.2 = (bf16[448,384]{1,0:T(8,128)(2,1)S(1)}, bf16[448,384]{1,0:T(8,128)(2,1)S(1)}, u32[]{:S(2)}, u32[]{:S(2)}) collective-permute-start(bf16[448,384]{1,0:T(8,128)(2,1)S(1)} %collective-permute-done), channel_id=1, source_target_pairs={{0,8},{8,16},{16,24},{24,32},{32,40},{40,48},{48,56},{56,0},{1,9},... | collective-permute-start | bytes 1032200 | tf_op jit(solution)/shard_map/ppermute | solution.py:315
  53.4 35.1 %collective-permute-start.10 = (bf16[128,3584]{1,0:T(8,128)(2,1)S(1)}, bf16[128,3584]{1,0:T(8,128)(2,1)}, u32[]{:S(2)}, u32[]{:S(2)}) collective-permute-start(bf16[128,3584]{1,0:T(8,128)(2,1)S(1)} %collective-permute-done.9.rest_11_), channel_id=1, source_target_pairs={{0,4},{4,0},{1,5},{5,1},{2,6},{6,2},{3,7},{7,3},{8,12},{12,8},{9,1... | collective-permute-start | bytes 2752520 | tf_op jit(solution)/shard_map/ppermute | solution.py:316
  54.0 34.5 %copy-start.5 = (bf16[448,384]{1,0:T(8,128)(2,1)}, bf16[448,384]{1,0:T(8,128)(2,1)S(1)}, u32[]{:S(2)}) copy-start(bf16[448,384]{1,0:T(8,128)(2,1)S(1)} %collective-permute-done.3) | copy-start | bytes 1032196
  54.0 34.5 %collective-permute-start.12 = (bf16[128,3584]{1,0:T(8,128)(2,1)S(1)}, bf16[128,3584]{1,0:T(8,128)(2,1)}, u32[]{:S(2)}, u32[]{:S(2)}) collective-permute-start(bf16[128,3584]{1,0:T(8,128)(2,1)S(1)} %collective-permute-done.11.rest_13_), channel_id=1, source_target_pairs={{0,4},{4,0},{1,5},{5,1},{2,6},{6,2},{3,7},{7,3},{8,12},{12,8},{9,1... | collective-permute-start | bytes 2752520 | tf_op jit(solution)/shard_map/ppermute | solution.py:316
  61.8 26.7 %copy-start.6 = (bf16[448,384]{1,0:T(8,128)(2,1)}, bf16[448,384]{1,0:T(8,128)(2,1)S(1)}, u32[]{:S(2)}) copy-start(bf16[448,384]{1,0:T(8,128)(2,1)S(1)} %collective-permute-done.2) | copy-start | bytes 1032196
  61.8 14.7 %collective-permute-start.5 = (bf16[448,384]{1,0:T(8,128)(2,1)S(1)}, bf16[448,384]{1,0:T(8,128)(2,1)}, u32[]{:S(2)}, u32[]{:S(2)}) collective-permute-start(bf16[448,384]{1,0:T(8,128)(2,1)S(1)} %collective-permute-done.3), channel_id=1, source_target_pairs={{0,56},{8,0},{16,8},{24,16},{32,24},{40,32},{48,40},{56,48},{1,57}... | collective-permute-start | bytes 1032200 | tf_op jit(solution)/shard_map/ppermute | solution.py:315
  61.9 12.6 %collective-permute-start.7 = (bf16[224,384]{1,0:T(8,128)(2,1)S(1)}, bf16[224,384]{1,0:T(8,128)(2,1)S(1)}, u32[]{:S(2)}, u32[]{:S(2)}) collective-permute-start(bf16[224,384]{1,0:T(8,128)(2,1)S(1)} %slice.46), channel_id=1, source_target_pairs={{0,48},{8,56},{16,0},{24,8},{32,16},{40,24},{48,32},{56,40},{1,49}... | collective-permute-start | bytes 516104 | tf_op jit(solution)/shard_map/ppermute | solution.py:315
  62.0 12.6 %collective-permute-start.6 = (bf16[224,384]{1,0:T(8,128)(2,1)S(1)}, bf16[224,384]{1,0:T(8,128)(2,1)S(1)}, u32[]{:S(2)}, u32[]{:S(2)}) collective-permute-start(bf16[224,384]{1,0:T(8,128)(2,1)S(1)} %slice.45), channel_id=1, source_target_pairs={{0,16},{8,24},{16,32},{24,40},{32,48},{40,56},{48,0},{56,8},{1,17}... | collective-permute-start | bytes 516104 | tf_op jit(solution)/shard_map/ppermute | solution.py:315
  74.6 13.9 %collective-permute-start.14 = (bf16[64,3584]{1,0:T(8,128)(2,1)}, bf16[64,3584]{1,0:T(8,128)(2,1)}, u32[]{:S(2)}, u32[]{:S(2)}) collective-permute-start(bf16[64,3584]{1,0:T(8,128)(2,1)} %collective-permute-done.13.rest_15_), channel_id=1, source_target_pairs={{0,4},{4,0},{1,5},{5,1},{2,6},{6,2},{3,7},{7,3},{8,12},{12,8},{9,1... | collective-permute-start | bytes 1376264 | tf_op jit(solution)/shard_map/ppermute | solution.py:316
  75.2 13.3 %collective-permute-start.16 = (bf16[64,3584]{1,0:T(8,128)(2,1)}, bf16[64,3584]{1,0:T(8,128)(2,1)}, u32[]{:S(2)}, u32[]{:S(2)}) collective-permute-start(bf16[64,3584]{1,0:T(8,128)(2,1)} %collective-permute-done.15.rest_17_), channel_id=1, source_target_pairs={{0,4},{4,0},{1,5},{5,1},{2,6},{6,2},{3,7},{7,3},{8,12},{12,8},{9,1... | collective-permute-start | bytes 1376264 | tf_op jit(solution)/shard_map/ppermute | solution.py:316
  76.5 12.0 %collective-permute-start.4 = (bf16[448,384]{1,0:T(8,128)(2,1)S(1)}, bf16[448,384]{1,0:T(8,128)(2,1)}, u32[]{:S(2)}, u32[]{:S(2)}) collective-permute-start(bf16[448,384]{1,0:T(8,128)(2,1)S(1)} %collective-permute-done.2), channel_id=1, source_target_pairs={{0,8},{8,16},{16,24},{24,32},{32,40},{40,48},{48,56},{56,0},{1,9},... | collective-permute-start | bytes 1032200 | tf_op jit(solution)/shard_map/ppermute | solution.py:315
  126.4 59.9 %copy-start = (s32[3]{0:T(128)S(1)}, s32[3]{0:T(128)}, u32[]{:S(2)}) copy-start(s32[3]{0:T(128)} %pad_add_fusion.ids) | copy-start | bytes 40
  162.7 19.5 %all-to-all-start.5 = ((bf16[32,112,128]{2,1,0:T(8,128)(2,1)}), bf16[32,112,128]{2,1,0:T(8,128)(2,1)S(1)}, u32[]{:S(2)}, u32[]{:S(2)}) async-start(bf16[32,112,128]{2,1,0:T(8,128)(2,1)} %get-tuple-element.20), calls=%async_computation.5 | async-start | bytes 1835008 | tf_op jit(solution)/shard_map/all_to_all | solution.py:412
  167.7 1.5 collective-permute-start.17
  170.0 16.3 %collective-permute-start.20 = (bf16[2,128,128]{2,1,0:T(8,128)(2,1)S(1)}, bf16[2,128,128]{2,1,0:T(8,128)(2,1)S(1)}, u32[]{:S(2)}, u32[]{:S(2)}) collective-permute-start(bf16[2,128,128]{2,1,0:T(8,128)(2,1)S(1)} %pad_maximum_fusion.1.pair), channel_id=1, source_target_pairs={{0,128},{64,192},{128,0},{192,64},{1,129},{65,193},{129,1},{193,65... | collective-permute-start | bytes 196616 | tf_op jit(solution)/shard_map/ppermute | solution.py:315
  172.9 13.3 %collective-permute-start.19 = (bf16[2,128,128]{2,1,0:T(8,128)(2,1)S(1)}, bf16[2,128,128]{2,1,0:T(8,128)(2,1)S(1)}, u32[]{:S(2)}, u32[]{:S(2)}) collective-permute-start(bf16[2,128,128]{2,1,0:T(8,128)(2,1)S(1)} %pad_maximum_fusion.1.pair), channel_id=1, source_target_pairs={{0,192},{64,0},{128,64},{192,128},{1,193},{65,1},{129,65},{193,129... | collective-permute-start | bytes 196616 | tf_op jit(solution)/shard_map/ppermute | solution.py:315
  174.1 12.2 %collective-permute-start.18 = (bf16[2,128,128]{2,1,0:T(8,128)(2,1)S(1)}, bf16[2,128,128]{2,1,0:T(8,128)(2,1)S(1)}, u32[]{:S(2)}, u32[]{:S(2)}) collective-permute-start(bf16[2,128,128]{2,1,0:T(8,128)(2,1)S(1)} %pad_maximum_fusion.1.pair), channel_id=1, source_target_pairs={{0,64},{64,128},{128,192},{192,0},{1,65},{65,129},{129,193},{193,1... | collective-permute-start | bytes 196616 | tf_op jit(solution)/shard_map/ppermute | solution.py:315
  182.9 11.3 %all-to-all-start.6 = ((bf16[8,16,128]{2,1,0:T(8,128)(2,1)}), bf16[8,16,128]{2,1,0:T(8,128)(2,1)S(1)}, u32[]{:S(2)}, u32[]{:S(2)}) async-start(bf16[8,16,128]{2,1,0:T(8,128)(2,1)} %shard_map.101), calls=%async_computation.6 | async-start | bytes 65536 | tf_op jit(solution)/shard_map/all_to_all | solution.py:419
  (3 other events, 9.8 us)
where the time goes:
time: 196 us; the launch traced here: 195 us
  waiting for transfers between devices  71.1 us (36%)
  blocking collectives  50.8 us (26%)
  starting transfers between devices  37.4 us (19%)
  Pallas kernels  28.1 us (14%)
  local copies, waits for them, and re-layouts  4.45 us (2%)
  other arithmetic  1.99 us (1%)
    ppermute x15, waiting for transfers between devices, layer(): lax.ppermute(v, a, [(i, (i + s) % n) for i in range(n)])  33.8 us
    pallas_call x9, Pallas kernels, call(): pl.pallas_call(kernel, out_shape=outs, in_specs=specs or [VMEM] * len(arg...  28.1 us
    all_to_all x2, blocking collectives, layer(): got = lax.all_to_all(send, 'z', 0, 0, tiled=True)  26.2 us
    ppermute x15, starting transfers between devices, layer(): lax.ppermute(v, a, [(i, (i + s) % n) for i in range(n)])  24.8 us
    all_to_all x1, waiting for transfers between devices, layer(): bundle = lax.all_to_all(bundle, group, 0, 0, tiled=True)  22.3 us
    all_to_all x1, blocking collectives, layer(): s_in = lax.all_to_all(scanned, 'z', 0, 0, tiled=True)  12.8 us
    all_to_all x1, blocking collectives, layer(): r_in = lax.all_to_all(scanned, 'z', 0, 0, tiled=True)  11.8 us
    all_to_all x1, waiting for transfers between devices, layer(): down_terms = lax.all_to_all(down_terms, ('y', 'c', 'x'), 0, 0, tiled=True)  7.17 us
  transfers between devices with their start and end apart: 24, of which 9 were waited for; matrix products, arithmetic and copies ran while one was open for 3% of the time, Pallas kernels for 2%

commit v1 on v0

--- a/solution.py
+++ b/solution.py
@@ -339,8 +339,9 @@
         behind = ring(behind, -1, "z", nz)
         weights += [ahead, behind]
     half = heads * rows // 2
-    weights.append(ring(weights[3][:half], 2, "z", nz))
-    weights.append(ring(weights[4][half:], -2, "z", nz))
+    upper, lower = weights[3][:half], weights[4][half:]
+    weights.append(ring(upper, 2, "z", nz))
+    weights.append(ring(lower, -2, "z", nz))
     deep = nc * rows
     weights = [p.reshape(-1, deep, 3 * hk) for p in weights]
 

time: 196 us -> 196 us (level)
  no operation moved by 1% of the time
where the time goes in v1:
time: 196 us; the launch traced here: 195 us
  waiting for transfers between devices  71.1 us (36%)
  blocking collectives  50.8 us (26%)
  starting transfers between devices  37.4 us (19%)
  Pallas kernels  28.1 us (14%)
  local copies, waits for them, and re-layouts  4.45 us (2%)
  other arithmetic  1.99 us (1%)
    ppermute x15, waiting for transfers between devices, layer(): lax.ppermute(v, a, [(i, (i + s) % n) for i in range(n)])  33.8 us
    pallas_call x9, Pallas kernels, call(): pl.pallas_call(kernel, out_shape=outs, in_specs=specs or [VMEM] * len(arg...  28.1 us
    all_to_all x2, blocking collectives, layer(): got = lax.all_to_all(send, 'z', 0, 0, tiled=True)  26.2 us
    ppermute x15, starting transfers between devices, layer(): lax.ppermute(v, a, [(i, (i + s) % n) for i in range(n)])  24.8 us
    all_to_all x1, waiting for transfers between devices, layer(): bundle = lax.all_to_all(bundle, group, 0, 0, tiled=True)  22.3 us
    all_to_all x1, blocking collectives, layer(): s_in = lax.all_to_all(scanned, 'z', 0, 0, tiled=True)  12.8 us
    all_to_all x1, blocking collectives, layer(): r_in = lax.all_to_all(scanned, 'z', 0, 0, tiled=True)  11.8 us
    all_to_all x1, waiting for transfers between devices, layer(): down_terms = lax.all_to_all(down_terms, ('y', 'c', 'x'), 0, 0, tiled=True)  7.17 us
  transfers between devices with their start and end apart: 24, of which 9 were waited for; matrix products, arithmetic and copies ran while one was open for 3% of the time, Pallas kernels for 2%

profile of v1, /device:TPU:2, one launch (start us, length us, event | category | flops | bytes accessed | tf_op | source)
XLA Modules:
  0.0 194.8 jit_solution(13971471230427062361)
XLA Ops:
  0.6 1.7 collective-permute-start.9
  2.3 1.7 collective-permute-start.11
  3.9 2.1 %shard_map.95 = bf16[8,104,384]{2,1,0:T(8,128)(2,1)} custom-call(bf16[56,1024]{1,0:T(8,128)(2,1)} %a_hbm.1, bf16[56,1024]{1,0:T(8,128)(2,1)} %b_hbm.1, bf16[56,1024]{1,0:T(8,128)(2,1)} %c_hbm.1, bf16[128,1024]{1,0:T(8,128)(2,1)} %grad_hbm.1, f32[8,128]{1,0:T(8,128)} %decay_hbm.1), custom_call_target="tpu_custom_call" | custom-call | tf_op jit(solution)/shard_map/pallas_call | solution.py:37
  6.0 3.6 %all-to-all-start = ((bf16[8,104,384]{2,1,0:T(8,128)(2,1)}), bf16[8,104,384]{2,1,0:T(8,128)(2,1)S(1)}, u32[]{:S(2)}, u32[]{:S(2)}) async-start(bf16[8,104,384]{2,1,0:T(8,128)(2,1)} %shard_map.95), calls=%async_computation | async-start | bytes 1277952 | tf_op jit(solution)/shard_map/all_to_all | solution.py:334
  10.0 22.3 %all-to-all-done.bundle_hbm = bf16[8,104,384]{2,1,0:T(8,128)(2,1)S(1)} async-done(((bf16[8,104,384]{2,1,0:T(8,128)(2,1)}), bf16[8,104,384]{2,1,0:T(8,128)(2,1)S(1)}, u32[]{:S(2)}, u32[]{:S(2)}) %all-to-all-start) | async-done | bytes 639008 | tf_op jit(solution)/shard_map/all_to_all | solution.py:334
  32.4 5.9 %collective-permute-start.1 = (bf16[448,384]{1,0:T(8,128)(2,1)S(1)}, bf16[448,384]{1,0:T(8,128)(2,1)S(1)}, u32[]{:S(2)}, u32[]{:S(2)}) collective-permute-start(bf16[448,384]{1,0:T(8,128)(2,1)S(1)} %bitcast.25), channel_id=1, source_target_pairs={{0,56},{8,0},{16,8},{24,16},{32,24},{40,32},{48,40},{56,48},{1,57}... | collective-permute-start | bytes 1032200 | tf_op jit(solution)/shard_map/ppermute | solution.py:315
  38.3 6.4 %collective-permute-done.1 = bf16[448,384]{1,0:T(8,128)(2,1)S(1)} collective-permute-done((bf16[448,384]{1,0:T(8,128)(2,1)S(1)}, bf16[448,384]{1,0:T(8,128)(2,1)S(1)}, u32[]{:S(2)}, u32[]{:S(2)}) %collective-permute-start.1) | collective-permute-done | bytes 344096 | tf_op jit(solution)/shard_map/ppermute | solution.py:315
  44.7 3.7 %collective-permute-start.3 = (bf16[448,384]{1,0:T(8,128)(2,1)S(1)}, bf16[448,384]{1,0:T(8,128)(2,1)S(1)}, u32[]{:S(2)}, u32[]{:S(2)}) collective-permute-start(bf16[448,384]{1,0:T(8,128)(2,1)S(1)} %collective-permute-done.1), channel_id=1, source_target_pairs={{0,56},{8,0},{16,8},{24,16},{32,24},{40,32},{48,40},{56,48},{1,57}... | collective-permute-start | bytes 1032200 | tf_op jit(solution)/shard_map/ppermute | solution.py:315
  48.4 0.8 slice.47
  49.3 1.1 collective-permute-start.13
  50.4 0.8 slice.48
  51.3 2.1 %collective-permute-start.15 = (bf16[64,3584]{1,0:T(8,128)(2,1)}, bf16[64,3584]{1,0:T(8,128)(2,1)}, u32[]{:S(2)}, u32[]{:S(2)}) collective-permute-start(bf16[64,3584]{1,0:T(8,128)(2,1)} %slice.48), channel_id=1, source_target_pairs={{0,192},{64,0},{128,64},{192,128},{1,193},{65,1},{129,65},{193,129... | collective-permute-start | bytes 1376264 | tf_op jit(solution)/shard_map/ppermute | solution.py:315
  54.0 7.8 %collective-permute-done.2 = bf16[448,384]{1,0:T(8,128)(2,1)S(1)} collective-permute-done((bf16[448,384]{1,0:T(8,128)(2,1)S(1)}, bf16[448,384]{1,0:T(8,128)(2,1)S(1)}, u32[]{:S(2)}, u32[]{:S(2)}) %collective-permute-start.2) | collective-permute-done | bytes 344096 | tf_op jit(solution)/shard_map/ppermute | solution.py:315
  62.0 2.9 %collective-permute-start.6 = (bf16[224,384]{1,0:T(8,128)(2,1)S(1)}, bf16[224,384]{1,0:T(8,128)(2,1)S(1)}, u32[]{:S(2)}, u32[]{:S(2)}) collective-permute-start(bf16[224,384]{1,0:T(8,128)(2,1)S(1)} %slice.45), channel_id=1, source_target_pairs={{0,16},{8,24},{16,32},{24,40},{32,48},{40,56},{48,0},{56,8},{1,17}... | collective-permute-start | bytes 516104 | tf_op jit(solution)/shard_map/ppermute | solution.py:315
  65.7 8.9 %collective-permute-done.7 = bf16[224,384]{1,0:T(8,128)(2,1)S(1)} collective-permute-done((bf16[224,384]{1,0:T(8,128)(2,1)S(1)}, bf16[224,384]{1,0:T(8,128)(2,1)S(1)}, u32[]{:S(2)}, u32[]{:S(2)}) %collective-permute-start.7) | collective-permute-done | bytes 172064 | tf_op jit(solution)/shard_map/ppermute | solution.py:315
  78.4 10.1 %collective-permute-done.4 = bf16[448,384]{1,0:T(8,128)(2,1)} collective-permute-done((bf16[448,384]{1,0:T(8,128)(2,1)S(1)}, bf16[448,384]{1,0:T(8,128)(2,1)}, u32[]{:S(2)}, u32[]{:S(2)}) %collective-permute-start.4) | collective-permute-done | bytes 344096 | tf_op jit(solution)/shard_map/ppermute | solution.py:315
  88.6 10.6 %shard_map.96 = (bf16[4,4,256,128]{3,2,1,0:T(8,128)(2,1)}, f32[4,256,128]{2,1,0:T(8,128)}, bf16[8,128,3584]{2,1,0:T(8,128)(2,1)}, bf16[8,112,128]{2,1,0:T(8,128)(2,1)}) custom-call(s32[3]{0:T(128)} %pad_add_fusion.ids, bf16[4,8,112,128]{3,2,1,0:T(8,128)(2,1)} %bitcast.28, bf16[4,112,384]{2,1,0:T(8,128)(2,1)} %bitcast.27, bf16[4,112,384]{2,1,0:T(8,128)(2,1)} %bitcast.33, ...), custom_call_target="tpu_custom_call" | custom-call | tf_op jit(solution)/shard_map/pallas_call | solution.py:37
  99.2 14.2 %all_to_all.35.got = bf16[8,112,128]{2,1,0:T(8,128)(2,1)S(1)} all-to-all(bf16[8,112,128]{2,1,0:T(8,128)(2,1)} %get-tuple-element.12), channel_id=1, replica_groups=mesh['y'=4,'z'=8,'c'=2,'x'=4] {'z'}, dimensions={0} | all-to-all | bytes 458752 | tf_op jit(solution)/shard_map/all_to_all | solution.py:374
  113.5 12.8 %all_to_all.36.s_in = bf16[8,96,128]{2,1,0:T(8,128)(2,1)} all-to-all(bf16[8,96,128]{2,1,0:T(8,128)(2,1)S(1)} %get-tuple-element.13), channel_id=1, replica_groups=mesh['y'=4,'z'=8,'c'=2,'x'=4] {'z'}, dimensions={0} | all-to-all | bytes 393216 | tf_op jit(solution)/shard_map/all_to_all | solution.py:376
  126.4 5.8 %shard_map.98 = (bf16[8,48,128]{2,1,0:T(8,128)(2,1)}, f32[4,256,128]{2,1,0:T(8,128)}) custom-call(bf16[8,96,128]{2,1,0:T(8,128)(2,1)} %all_to_all.36.s_in, bf16[2,128,128]{2,1,0:T(8,128)(2,1)} %pad_maximum_fusion.rest_19_.lift, f32[4,256]{1,0:T(4,128)} %add.26.rest_20_.logs, bf16[4,4,256,128]{3,2,1,0:T(8,128)(2,1)} %get-tuple-element.14.kvql_hbm, ...), custom_call_target="tpu_custom_call" | custom-call | tf_op jit(solution)/shard_map/pallas_call | solution.py:37
  132.1 12.0 %all_to_all.37.got = bf16[8,48,128]{2,1,0:T(8,128)(2,1)S(1)} all-to-all(bf16[8,48,128]{2,1,0:T(8,128)(2,1)} %get-tuple-element.16), channel_id=1, replica_groups=mesh['y'=4,'z'=8,'c'=2,'x'=4] {'z'}, dimensions={0} | all-to-all | bytes 196608 | tf_op jit(solution)/shard_map/all_to_all | solution.py:393
  144.2 11.8 %all_to_all.38.r_in = bf16[8,48,128]{2,1,0:T(8,128)(2,1)} all-to-all(bf16[8,48,128]{2,1,0:T(8,128)(2,1)S(1)} %shard_map.99), channel_id=1, replica_groups=mesh['y'=4,'z'=8,'c'=2,'x'=4] {'z'}, dimensions={0} | all-to-all | bytes 196608 | tf_op jit(solution)/shard_map/all_to_all | solution.py:395
  156.0 6.7 %shard_map.100 = (bf16[32,112,128]{2,1,0:T(8,128)(2,1)}, bf16[128,128]{1,0:T(8,128)(2,1)}) custom-call(bf16[8,48,128]{2,1,0:T(8,128)(2,1)} %all_to_all.38.r_in, f32[4,256]{1,0:T(4,128)} %add.26.rest_20_.logs, bf16[4,4,256,128]{3,2,1,0:T(8,128)(2,1)} %get-tuple-element.14.kvql_hbm, f32[4,256,128]{2,1,0:T(8,128)} %get-tuple-element.18.back_hbm, ...), custom_call_target="tpu_custom_call" | custom-call | tf_op jit(solution)/shard_map/pallas_call | solution.py:37
  162.7 5.0 %all-to-all-start.5 = ((bf16[32,112,128]{2,1,0:T(8,128)(2,1)}), bf16[32,112,128]{2,1,0:T(8,128)(2,1)S(1)}, u32[]{:S(2)}, u32[]{:S(2)}) async-start(bf16[32,112,128]{2,1,0:T(8,128)(2,1)} %get-tuple-element.20), calls=%async_computation.5 | async-start | bytes 1835008 | tf_op jit(solution)/shard_map/all_to_all | solution.py:413
  167.9 1.3 collective-permute-done.17
  170.0 3.0 %collective-permute-start.20 = (bf16[2,128,128]{2,1,0:T(8,128)(2,1)S(1)}, bf16[2,128,128]{2,1,0:T(8,128)(2,1)S(1)}, u32[]{:S(2)}, u32[]{:S(2)}) collective-permute-start(bf16[2,128,128]{2,1,0:T(8,128)(2,1)S(1)} %pad_maximum_fusion.1.pair), channel_id=1, source_target_pairs={{0,128},{64,192},{128,0},{192,64},{1,129},{65,193},{129,1},{193,65... | collective-permute-start | bytes 196616 | tf_op jit(solution)/shard_map/ppermute | solution.py:315
  172.9 1.2 collective-permute-start.19
  174.1 0.9 collective-permute-start.18
  175.0 7.2 %all-to-all-done.5.got = bf16[32,112,128]{2,1,0:T(8,128)(2,1)S(1)} async-done(((bf16[32,112,128]{2,1,0:T(8,128)(2,1)}), bf16[32,112,128]{2,1,0:T(8,128)(2,1)S(1)}, u32[]{:S(2)}, u32[]{:S(2)}) %all-to-all-start.5) | async-done | bytes 917536 | tf_op jit(solution)/shard_map/all_to_all | solution.py:413
  182.9 3.3 %all-to-all-start.6 = ((bf16[8,16,128]{2,1,0:T(8,128)(2,1)}), bf16[8,16,128]{2,1,0:T(8,128)(2,1)S(1)}, u32[]{:S(2)}, u32[]{:S(2)}) async-start(bf16[8,16,128]{2,1,0:T(8,128)(2,1)} %shard_map.101), calls=%async_computation.6 | async-start | bytes 65536 | tf_op jit(solution)/shard_map/all_to_all | solution.py:420
  186.3 1.4 shard_map.103
  187.7 6.5 %all-to-all-done.6.got = bf16[8,16,128]{2,1,0:T(8,128)(2,1)S(1)} async-done(((bf16[8,16,128]{2,1,0:T(8,128)(2,1)}), bf16[8,16,128]{2,1,0:T(8,128)(2,1)S(1)}, u32[]{:S(2)}, u32[]{:S(2)}) %all-to-all-start.6) | async-done | bytes 32800 | tf_op jit(solution)/shard_map/all_to_all | solution.py:420
  (64 shorter events, 8.4 us)
Async XLA Ops:
  0.6 47.8 %collective-permute-start.9 = (bf16[128,3584]{1,0:T(8,128)(2,1)}, bf16[128,3584]{1,0:T(8,128)(2,1)S(1)}, u32[]{:S(2)}, u32[]{:S(2)}) collective-permute-start(bf16[128,3584]{1,0:T(8,128)(2,1)} %rest_9_.1), channel_id=1, source_target_pairs={{0,64},{64,128},{128,192},{192,0},{1,65},{65,129},{129,193},{193,1... | collective-permute-start | bytes 2752520 | tf_op jit(solution)/shard_map/ppermute | solution.py:315
  2.3 48.1 %collective-permute-start.11 = (bf16[128,3584]{1,0:T(8,128)(2,1)}, bf16[128,3584]{1,0:T(8,128)(2,1)S(1)}, u32[]{:S(2)}, u32[]{:S(2)}) collective-permute-start(bf16[128,3584]{1,0:T(8,128)(2,1)} %rest_9_.1), channel_id=1, source_target_pairs={{0,192},{64,0},{128,64},{192,128},{1,193},{65,1},{129,65},{193,129... | collective-permute-start | bytes 2752520 | tf_op jit(solution)/shard_map/ppermute | solution.py:315
  6.0 26.3 %all-to-all-start = ((bf16[8,104,384]{2,1,0:T(8,128)(2,1)}), bf16[8,104,384]{2,1,0:T(8,128)(2,1)S(1)}, u32[]{:S(2)}, u32[]{:S(2)}) async-start(bf16[8,104,384]{2,1,0:T(8,128)(2,1)} %shard_map.95), calls=%async_computation | async-start | bytes 1277952 | tf_op jit(solution)/shard_map/all_to_all | solution.py:334
  9.6 43.8 %collective-permute-start.8 = (bf16[128,3584]{1,0:T(8,128)(2,1)}, bf16[128,3584]{1,0:T(8,128)(2,1)}, u32[]{:S(2)}, u32[]{:S(2)}) collective-permute-start(bf16[128,3584]{1,0:T(8,128)(2,1)} %rest_9_.1), channel_id=1, source_target_pairs={{0,4},{4,0},{1,5},{5,1},{2,6},{6,2},{3,7},{7,3},{8,12},{12,8},{9,1... | collective-permute-start | bytes 2752520 | tf_op jit(solution)/shard_map/ppermute | solution.py:316
  32.3 66.9 %copy-start.1 = (bf16[8,104,384]{2,1,0:T(8,128)(2,1)}, bf16[8,104,384]{2,1,0:T(8,128)(2,1)S(1)}, u32[]{:S(2)}) copy-start(bf16[8,104,384]{2,1,0:T(8,128)(2,1)S(1)} %all-to-all-done.bundle_hbm) | copy-start | bytes 1916932
  32.3 56.2 %copy-start.4 = (bf16[8,56,384]{2,1,0:T(8,128)(2,1)}, bf16[8,56,384]{2,1,0:T(8,128)(2,1)S(1)}, u32[]{:S(2)}) copy-start(bf16[8,56,384]{2,1,0:T(8,128)(2,1)S(1)} %slice.44) | copy-start | bytes 1032196
  32.4 12.4 %collective-permute-start.1 = (bf16[448,384]{1,0:T(8,128)(2,1)S(1)}, bf16[448,384]{1,0:T(8,128)(2,1)S(1)}, u32[]{:S(2)}, u32[]{:S(2)}) collective-permute-start(bf16[448,384]{1,0:T(8,128)(2,1)S(1)} %bitcast.25), channel_id=1, source_target_pairs={{0,56},{8,0},{16,8},{24,16},{32,24},{40,32},{48,40},{56,48},{1,57}... | collective-permute-start | bytes 1032200 | tf_op jit(solution)/shard_map/ppermute | solution.py:315
  38.3 15.1 %collective-permute-start = (bf16[448,384]{1,0:T(8,128)(2,1)S(1)}, bf16[448,384]{1,0:T(8,128)(2,1)S(1)}, u32[]{:S(2)}, u32[]{:S(2)}) collective-permute-start(bf16[448,384]{1,0:T(8,128)(2,1)S(1)} %bitcast.26), channel_id=1, source_target_pairs={{0,8},{8,16},{16,24},{24,32},{32,40},{40,48},{48,56},{56,0},{1,9},... | collective-permute-start | bytes 1032200 | tf_op jit(solution)/shard_map/ppermute | solution.py:315
  44.7 17.1 %copy-start.7 = (bf16[448,384]{1,0:T(8,128)(2,1)}, bf16[448,384]{1,0:T(8,128)(2,1)S(1)}, u32[]{:S(2)}) copy-start(bf16[448,384]{1,0:T(8,128)(2,1)S(1)} %collective-permute-done.1) | copy-start | bytes 1032196
  44.7 9.3 %collective-permute-start.3 = (bf16[448,384]{1,0:T(8,128)(2,1)S(1)}, bf16[448,384]{1,0:T(8,128)(2,1)S(1)}, u32[]{:S(2)}, u32[]{:S(2)}) collective-permute-start(bf16[448,384]{1,0:T(8,128)(2,1)S(1)} %collective-permute-done.1), channel_id=1, source_target_pairs={{0,56},{8,0},{16,8},{24,16},{32,24},{40,32},{48,40},{56,48},{1,57}... | collective-permute-start | bytes 1032200 | tf_op jit(solution)/shard_map/ppermute | solution.py:315
  48.4 40.1 %copy-start.2 = (bf16[128,3584]{1,0:T(8,128)(2,1)}, bf16[128,3584]{1,0:T(8,128)(2,1)S(1)}, u32[]{:S(2)}) copy-start(bf16[128,3584]{1,0:T(8,128)(2,1)S(1)} %collective-permute-done.9.rest_11_) | copy-start | bytes 2752516
  49.3 12.6 %collective-permute-start.13 = (bf16[64,3584]{1,0:T(8,128)(2,1)}, bf16[64,3584]{1,0:T(8,128)(2,1)}, u32[]{:S(2)}, u32[]{:S(2)}) collective-permute-start(bf16[64,3584]{1,0:T(8,128)(2,1)} %slice.47), channel_id=1, source_target_pairs={{0,64},{64,128},{128,192},{192,0},{1,65},{65,129},{129,193},{193,1... | collective-permute-start | bytes 1376264 | tf_op jit(solution)/shard_map/ppermute | solution.py:315
  50.4 38.1 %copy-start.3 = (bf16[128,3584]{1,0:T(8,128)(2,1)}, bf16[128,3584]{1,0:T(8,128)(2,1)S(1)}, u32[]{:S(2)}) copy-start(bf16[128,3584]{1,0:T(8,128)(2,1)S(1)} %collective-permute-done.11.rest_13_) | copy-start | bytes 2752516
  51.3 10.8 %collective-permute-start.15 = (bf16[64,3584]{1,0:T(8,128)(2,1)}, bf16[64,3584]{1,0:T(8,128)(2,1)}, u32[]{:S(2)}, u32[]{:S(2)}) collective-permute-start(bf16[64,3584]{1,0:T(8,128)(2,1)} %slice.48), channel_id=1, source_target_pairs={{0,192},{64,0},{128,64},{192,128},{1,193},{65,1},{129,65},{193,129... | collective-permute-start | bytes 1376264 | tf_op jit(solution)/shard_map/ppermute | solution.py:315
  53.4 8.5 %collective-permute-start.2 = (bf16[448,384]{1,0:T(8,128)(2,1)S(1)}, bf16[448,384]{1,0:T(8,128)(2,1)S(1)}, u32[]{:S(2)}, u32[]{:S(2)}) collective-permute-start(bf16[448,384]{1,0:T(8,128)(2,1)S(1)} %collective-permute-done), channel_id=1, source_target_pairs={{0,8},{8,16},{16,24},{24,32},{32,40},{40,48},{48,56},{56,0},{1,9},... | collective-permute-start | bytes 1032200 | tf_op jit(solution)/shard_map/ppermute | solution.py:315
  53.4 35.1 %collective-permute-start.10 = (bf16[128,3584]{1,0:T(8,128)(2,1)S(1)}, bf16[128,3584]{1,0:T(8,128)(2,1)}, u32[]{:S(2)}, u32[]{:S(2)}) collective-permute-start(bf16[128,3584]{1,0:T(8,128)(2,1)S(1)} %collective-permute-done.9.rest_11_), channel_id=1, source_target_pairs={{0,4},{4,0},{1,5},{5,1},{2,6},{6,2},{3,7},{7,3},{8,12},{12,8},{9,1... | collective-permute-start | bytes 2752520 | tf_op jit(solution)/shard_map/ppermute | solution.py:316
  54.0 34.5 %copy-start.5 = (bf16[448,384]{1,0:T(8,128)(2,1)}, bf16[448,384]{1,0:T(8,128)(2,1)S(1)}, u32[]{:S(2)}) copy-start(bf16[448,384]{1,0:T(8,128)(2,1)S(1)} %collective-permute-done.3) | copy-start | bytes 1032196
  54.0 34.5 %collective-permute-start.12 = (bf16[128,3584]{1,0:T(8,128)(2,1)S(1)}, bf16[128,3584]{1,0:T(8,128)(2,1)}, u32[]{:S(2)}, u32[]{:S(2)}) collective-permute-start(bf16[128,3584]{1,0:T(8,128)(2,1)S(1)} %collective-permute-done.11.rest_13_), channel_id=1, source_target_pairs={{0,4},{4,0},{1,5},{5,1},{2,6},{6,2},{3,7},{7,3},{8,12},{12,8},{9,1... | collective-permute-start | bytes 2752520 | tf_op jit(solution)/shard_map/ppermute | solution.py:316
  61.8 26.7 %copy-start.6 = (bf16[448,384]{1,0:T(8,128)(2,1)}, bf16[448,384]{1,0:T(8,128)(2,1)S(1)}, u32[]{:S(2)}) copy-start(bf16[448,384]{1,0:T(8,128)(2,1)S(1)} %collective-permute-done.2) | copy-start | bytes 1032196
  61.8 14.7 %collective-permute-start.5 = (bf16[448,384]{1,0:T(8,128)(2,1)S(1)}, bf16[448,384]{1,0:T(8,128)(2,1)}, u32[]{:S(2)}, u32[]{:S(2)}) collective-permute-start(bf16[448,384]{1,0:T(8,128)(2,1)S(1)} %collective-permute-done.3), channel_id=1, source_target_pairs={{0,56},{8,0},{16,8},{24,16},{32,24},{40,32},{48,40},{56,48},{1,57}... | collective-permute-start | bytes 1032200 | tf_op jit(solution)/shard_map/ppermute | solution.py:315
  61.9 12.6 %collective-permute-start.7 = (bf16[224,384]{1,0:T(8,128)(2,1)S(1)}, bf16[224,384]{1,0:T(8,128)(2,1)S(1)}, u32[]{:S(2)}, u32[]{:S(2)}) collective-permute-start(bf16[224,384]{1,0:T(8,128)(2,1)S(1)} %slice.46), channel_id=1, source_target_pairs={{0,48},{8,56},{16,0},{24,8},{32,16},{40,24},{48,32},{56,40},{1,49}... | collective-permute-start | bytes 516104 | tf_op jit(solution)/shard_map/ppermute | solution.py:315
  62.0 12.6 %collective-permute-start.6 = (bf16[224,384]{1,0:T(8,128)(2,1)S(1)}, bf16[224,384]{1,0:T(8,128)(2,1)S(1)}, u32[]{:S(2)}, u32[]{:S(2)}) collective-permute-start(bf16[224,384]{1,0:T(8,128)(2,1)S(1)} %slice.45), channel_id=1, source_target_pairs={{0,16},{8,24},{16,32},{24,40},{32,48},{40,56},{48,0},{56,8},{1,17}... | collective-permute-start | bytes 516104 | tf_op jit(solution)/shard_map/ppermute | solution.py:315
  74.6 13.9 %collective-permute-start.14 = (bf16[64,3584]{1,0:T(8,128)(2,1)}, bf16[64,3584]{1,0:T(8,128)(2,1)}, u32[]{:S(2)}, u32[]{:S(2)}) collective-permute-start(bf16[64,3584]{1,0:T(8,128)(2,1)} %collective-permute-done.13.rest_15_), channel_id=1, source_target_pairs={{0,4},{4,0},{1,5},{5,1},{2,6},{6,2},{3,7},{7,3},{8,12},{12,8},{9,1... | collective-permute-start | bytes 1376264 | tf_op jit(solution)/shard_map/ppermute | solution.py:316
  75.2 13.3 %collective-permute-start.16 = (bf16[64,3584]{1,0:T(8,128)(2,1)}, bf16[64,3584]{1,0:T(8,128)(2,1)}, u32[]{:S(2)}, u32[]{:S(2)}) collective-permute-start(bf16[64,3584]{1,0:T(8,128)(2,1)} %collective-permute-done.15.rest_17_), channel_id=1, source_target_pairs={{0,4},{4,0},{1,5},{5,1},{2,6},{6,2},{3,7},{7,3},{8,12},{12,8},{9,1... | collective-permute-start | bytes 1376264 | tf_op jit(solution)/shard_map/ppermute | solution.py:316
  76.5 12.0 %collective-permute-start.4 = (bf16[448,384]{1,0:T(8,128)(2,1)S(1)}, bf16[448,384]{1,0:T(8,128)(2,1)}, u32[]{:S(2)}, u32[]{:S(2)}) collective-permute-start(bf16[448,384]{1,0:T(8,128)(2,1)S(1)} %collective-permute-done.2), channel_id=1, source_target_pairs={{0,8},{8,16},{16,24},{24,32},{32,40},{40,48},{48,56},{56,0},{1,9},... | collective-permute-start | bytes 1032200 | tf_op jit(solution)/shard_map/ppermute | solution.py:315
  126.4 59.9 %copy-start = (s32[3]{0:T(128)S(1)}, s32[3]{0:T(128)}, u32[]{:S(2)}) copy-start(s32[3]{0:T(128)} %pad_add_fusion.ids) | copy-start | bytes 40
  162.7 19.5 %all-to-all-start.5 = ((bf16[32,112,128]{2,1,0:T(8,128)(2,1)}), bf16[32,112,128]{2,1,0:T(8,128)(2,1)S(1)}, u32[]{:S(2)}, u32[]{:S(2)}) async-start(bf16[32,112,128]{2,1,0:T(8,128)(2,1)} %get-tuple-element.20), calls=%async_computation.5 | async-start | bytes 1835008 | tf_op jit(solution)/shard_map/all_to_all | solution.py:413
  167.7 1.5 collective-permute-start.17
  170.0 16.3 %collective-permute-start.20 = (bf16[2,128,128]{2,1,0:T(8,128)(2,1)S(1)}, bf16[2,128,128]{2,1,0:T(8,128)(2,1)S(1)}, u32[]{:S(2)}, u32[]{:S(2)}) collective-permute-start(bf16[2,128,128]{2,1,0:T(8,128)(2,1)S(1)} %pad_maximum_fusion.1.pair), channel_id=1, source_target_pairs={{0,128},{64,192},{128,0},{192,64},{1,129},{65,193},{129,1},{193,65... | collective-permute-start | bytes 196616 | tf_op jit(solution)/shard_map/ppermute | solution.py:315
  172.9 13.3 %collective-permute-start.19 = (bf16[2,128,128]{2,1,0:T(8,128)(2,1)S(1)}, bf16[2,128,128]{2,1,0:T(8,128)(2,1)S(1)}, u32[]{:S(2)}, u32[]{:S(2)}) collective-permute-start(bf16[2,128,128]{2,1,0:T(8,128)(2,1)S(1)} %pad_maximum_fusion.1.pair), channel_id=1, source_target_pairs={{0,192},{64,0},{128,64},{192,128},{1,193},{65,1},{129,65},{193,129... | collective-permute-start | bytes 196616 | tf_op jit(solution)/shard_map/ppermute | solution.py:315
  174.1 12.2 %collective-permute-start.18 = (bf16[2,128,128]{2,1,0:T(8,128)(2,1)S(1)}, bf16[2,128,128]{2,1,0:T(8,128)(2,1)S(1)}, u32[]{:S(2)}, u32[]{:S(2)}) collective-permute-start(bf16[2,128,128]{2,1,0:T(8,128)(2,1)S(1)} %pad_maximum_fusion.1.pair), channel_id=1, source_target_pairs={{0,64},{64,128},{128,192},{192,0},{1,65},{65,129},{129,193},{193,1... | collective-permute-start | bytes 196616 | tf_op jit(solution)/shard_map/ppermute | solution.py:315
  182.9 11.3 %all-to-all-start.6 = ((bf16[8,16,128]{2,1,0:T(8,128)(2,1)}), bf16[8,16,128]{2,1,0:T(8,128)(2,1)S(1)}, u32[]{:S(2)}, u32[]{:S(2)}) async-start(bf16[8,16,128]{2,1,0:T(8,128)(2,1)} %shard_map.101), calls=%async_computation.6 | async-start | bytes 65536 | tf_op jit(solution)/shard_map/all_to_all | solution.py:420
  (3 other events, 9.8 us)
